TPU v7x, 32 devices: a whole 2x2x4 slice. The times are simulated.
32 devices in a mesh: obs: 2 (over x), snap: 16 (over z, y, core).
Axes of the slice: x: 2, y: 2, z: 4, core: 2. Of those that a mesh axis runs over, the one named last changes fastest.
Arguments:
- psi_x: bfloat16 [4096, 8192], P('snap', 'obs'), may hold values from -6 to 6
- psi_y: bfloat16 [4096, 8192], P('snap', 'obs'), may hold values from -6 to 6
- pattern: int32 [64, 64], P('obs'), may hold values from 0 to 1, as said below
Outputs:
- cross: float32 [32768, 128], P(('obs', 'snap'))
- whitened: float32 [2, 4096, 8192], P(None, 'snap', 'obs')
Inputs may be any that keep to these rules, and one draw needn't show every extreme that they name: Each row of pattern holds exactly 4 ones, the rest zeros.
All inputs are finite; a program needn't handle non-finite values.
Results may differ from a plain program's by a relative error of at most 0.0003.
Values may be sent and summed in bfloat16 or wider, within the bound.
A program may use at most 64 MiB of HBM per device.

v0:
```python
import functools
import math

import jax
import jax.numpy as jnp
from jax import lax
from jax.experimental import pallas as pl
from jax.experimental.pallas import tpu as pltpu
from jax.sharding import PartitionSpec as P

NNZ = 4


def passed_along(block, axis, distance):
    devices = range(lax.axis_size(axis))
    route = [((i - distance) % len(devices), i) for i in devices]
    return lax.ppermute(block, axis, route)


def general_shards(psi_x, psi_y, pattern):
    highest = lax.Precision.HIGHEST
    snap_rows = psi_x.shape[0]
    obs_width = psi_x.shape[1]
    local_blocks = pattern.shape[0]
    block_size = obs_width // local_blocks
    obs_count = lax.axis_size("obs")
    snap_count = lax.axis_size("snap")
    obs_index = lax.axis_index("obs")
    snap_total = snap_rows * snap_count
    total_blocks = pattern.shape[1]
    ranking = jnp.cumsum(pattern, axis=1) - 1
    slot_table = (
        (pattern[:, None, :] == 1)
        & (ranking[:, None, :] == jnp.arange(NNZ, dtype=jnp.int32)[None, :, None])
    ).astype(jnp.int32)
    columns = jnp.sum(slot_table * jnp.arange(total_blocks, dtype=jnp.int32)[None, None, :], axis=2)
    wanted = columns.reshape(local_blocks * NNZ)
    x_blocks = psi_x.reshape(snap_rows, local_blocks, block_size)
    y_blocks = psi_y.reshape(snap_rows, local_blocks, block_size)
    panels = [psi_y]
    sources = [obs_index]
    panel = psi_y
    for distance in range(1, obs_count):
        panel = passed_along(panel, "obs", 1)
        panels.append(panel)
        sources.append((obs_index - distance) % obs_count)
    panel_count = len(panels)
    stacked = jnp.stack(panels, axis=1).reshape(snap_rows, panel_count * local_blocks, block_size)
    source_list = jnp.stack(sources)
    global_of = (
        source_list[:, None] * local_blocks + jnp.arange(local_blocks, dtype=jnp.int32)[None, :]
    ).reshape(panel_count * local_blocks)
    select = (wanted[:, None] == global_of[None, :]).astype(jnp.bfloat16)
    chosen = jnp.einsum("spb,mp->smb", stacked, select, preferred_element_type=jnp.float32).astype(
        jnp.bfloat16
    )
    chosen = chosen.reshape(snap_rows, local_blocks, NNZ, block_size)
    product = jnp.einsum("sia,sikb->ikab", x_blocks, chosen, preferred_element_type=jnp.float32)
    partial_cross = (product * (1.0 / math.sqrt(snap_total))).reshape(
        local_blocks * NNZ * block_size, block_size
    )
    cross = lax.psum_scatter(partial_cross, "snap", scatter_dimension=0, tiled=True)
    gram = jnp.einsum("sia,sib->iab", x_blocks, x_blocks, preferred_element_type=jnp.float32)
    gram = gram + jnp.einsum("sia,sib->iab", y_blocks, y_blocks, preferred_element_type=jnp.float32)
    total_gram = lax.psum(gram, "snap")
    lower = jnp.linalg.cholesky(total_gram)
    identity = jnp.broadcast_to(
        jnp.eye(block_size, dtype=jnp.float32), (local_blocks, block_size, block_size)
    )
    inverse = lax.linalg.triangular_solve(lower, identity, left_side=True, lower=True)
    factor = math.sqrt(2.0 * snap_total)

    def whiten(blocks):
        mapped = jnp.einsum("sic,iac->sia", blocks.astype(jnp.float32), inverse, precision=highest)
        return (factor * mapped).reshape(snap_rows, obs_width)

    whitened = jnp.stack([whiten(x_blocks), whiten(y_blocks)])
    return (cross, whitened)


def dot_rows(a, b):
    return lax.dot_general(a, b, (((0,), (0,)), ((), ())), preferred_element_type=jnp.float32)


def kept_columns(pattern):
    total = pattern.shape[1]
    upper = jnp.triu(jnp.ones((total, total), jnp.bfloat16))
    counts = jnp.dot(pattern.astype(jnp.bfloat16), upper, preferred_element_type=jnp.float32)
    slots = jnp.arange(NNZ, dtype=jnp.float32)
    return jnp.sum((counts[:, None, :] <= slots[None, :, None] + 0.5).astype(jnp.int32), axis=2)


def place_of(position, snaps):
    depth = snaps // 4
    return (position % depth) * 4 + ((position // depth) % 2) * 2 + position // (2 * depth)


def pack_pair(first, second):
    bs = first.shape[0]
    row = lax.broadcasted_iota(jnp.int32, (bs, bs), 0)
    lane = lax.broadcasted_iota(jnp.int32, (bs, bs), 1)
    diagonal = jnp.sum(jnp.where(row == lane, second, 0.0), axis=0, keepdims=True)
    return jnp.where(lane <= row, first, second), jnp.broadcast_to(diagonal, (8, bs))


def eliminate(state_ref, first, last):
    count, bs, _ = state_ref.shape
    slab_count = bs // 8
    lanes = lax.broadcasted_iota(jnp.int32, (8, bs), 1)
    rows = lax.broadcasted_iota(jnp.int32, (8, bs), 0)

    def group(g, state):
        blocks = [list(state[n * slab_count : (n + 1) * slab_count]) for n in range(count)]
        for r in range(8):
            at_lane = lanes == r
            for block in blocks:
                pivot = 1.0 / block[0][r : r + 1, r : r + 1]
                scaled = jnp.where(at_lane[:1], pivot, block[0][r : r + 1, :] * pivot)
                for v in range(slab_count):
                    column = jnp.broadcast_to(block[v][:, r : r + 1], (8, bs))
                    updated = jnp.where(at_lane, 0.0, block[v]) - column * scaled
                    if v == 0:
                        block[v] = jnp.where(rows > r, updated, block[v])
                    else:
                        block[v] = jnp.where(v + g < slab_count, updated, block[v])
        turned = []
        for block in blocks:
            turned += [pltpu.roll(slab, bs - 8, 1) for slab in block[1:] + block[:1]]
        return tuple(turned)

    state = tuple(state_ref[n, 8 * v : 8 * v + 8, :] for n in range(count) for v in range(slab_count))
    state = lax.fori_loop(first, last, group, state)
    for n in range(count):
        for v in range(slab_count):
            state_ref[n, 8 * v : 8 * v + 8, :] = state[n * slab_count + v]


def scaled_rows(state):
    bs = state.shape[0]
    rows = lax.broadcasted_iota(jnp.int32, (bs, bs), 0)
    lanes = lax.broadcasted_iota(jnp.int32, (bs, bs), 1)
    pivot = jnp.sum(jnp.where(lanes == rows, state, 0.0), axis=1, keepdims=True)
    unit = jnp.where(lanes < rows, state, jnp.where(lanes == rows, 1.0, 0.0))
    return unit * (1.0 / jnp.sqrt(pivot))


def window_kernel(
    snaps, chunks, cross_scale, white_scale,
    columns_ref, x_ref, y_ref, cross_ref, inverse_ref,
    panels, partial, core_in, core_sum, y_out, y_in, y_sum, z_out, z_in, z_sum,
    y_out_scale, y_in_scale, z_out_scale, z_in_scale,
    gram, gram_core, gram_sum, gram_y, gram_ysum, gram_z, state, inverses,
    send_sem, recv_sem,
):
    rows, width = x_ref.shape
    bs = cross_ref.shape[1]
    blocks = width // bs
    depth = snaps // 4
    part = bs // chunks
    here = lax.axis_index("snap")
    side = lax.axis_index("obs")
    core, yy, zz = here % 2, (here // 2) % 2, here // 4
    to_x = (1 - side, here)
    to_core = (side, here + 1 - 2 * core)
    to_y = (side, here + 2 - 4 * yy)
    to_z = [(side, (here + 4 * m) % snaps) for m in range(1, depth)]
    mine = core * 2 * depth + yy * depth + zz

    barrier = pltpu.get_barrier_semaphore()
    others = [to_x, to_core, to_y] + to_z
    for device in others:
        pl.semaphore_signal(barrier, inc=1, device_id=device, device_id_type=pl.DeviceIdType.MESH)
    pl.semaphore_wait(barrier, len(others))

    started = []

    def send(src, dst, device):
        n = len(started)
        copy = pltpu.make_async_remote_copy(
            src_ref=src, dst_ref=dst, send_sem=send_sem.at[n], recv_sem=recv_sem.at[n],
            device_id=device, device_id_type=pl.DeviceIdType.MESH,
        )
        copy.start()
        started.append(copy)
        return copy

    @pl.loop(0, blocks)
    def _(j):
        turned = y_ref[:, pl.ds(pl.multiple_of(j * bs, bs), bs)].T
        for q in range(chunks):
            panels[q][j] = turned[q * part : (q + 1) * part]

    x_copies = [
        send(panels[q].at[pl.ds(0, blocks)], panels[q].at[pl.ds(blocks, blocks)], to_x) for q in range(chunks)
    ]

    @pl.loop(0, snaps)
    def _(position):
        pair = place_of(position, snaps)
        found = []
        for n in range(2):
            cut = pl.ds(pl.multiple_of((2 * pair + n) * bs, bs), bs)
            both = jnp.concatenate([x_ref[:, cut], y_ref[:, cut]], axis=0)
            found.append(dot_rows(both, both))
        packed, diagonal = pack_pair(*found)
        gram[position, :bs, :] = packed
        gram[position, bs:, :] = diagonal

    def add(out, count, a, a_first, b):
        @pl.loop(0, count)
        def _(n):
            out[n] = a[a_first + n] + b[n]

    gram_copy = send(gram.at[pl.ds((1 - core) * 2 * depth, 2 * depth)], gram_core, to_core)

    def gram_to_y():
        gram_copy.wait_recv()
        add(gram_sum, 2 * depth, gram, core * 2 * depth, gram_core)
        return send(gram_sum.at[pl.ds((1 - yy) * depth, depth)], gram_y, to_y)

    def gram_to_z(copy):
        copy.wait_recv()
        add(gram_ysum, depth, gram_sum, yy * depth, gram_y)
        return [send(gram_ysum.at[(zz + m) % depth], gram_z.at[m - 1], to_z[m - 1]) for m in range(1, depth)]

    def factor_start(copies):
        for copy in copies:
            copy.wait_recv()
        total = gram_ysum[zz]
        for m in range(depth - 1):
            total = total + gram_z[m]
        packed = total[:bs]
        row = lax.broadcasted_iota(jnp.int32, (bs, bs), 0)
        lane = lax.broadcasted_iota(jnp.int32, (bs, bs), 1)
        turned = packed.T
        first = jnp.where(lane <= row, packed, turned)
        second = jnp.where(lane > row, packed, jnp.where(lane < row, turned, jnp.broadcast_to(total[bs : bs + 1], (bs, bs))))
        state[0] = first
        state[1] = second

    def factor_end():
        low, high = scaled_rows(state[0]), scaled_rows(state[1])
        packed, diagonal = pack_pair(low * white_scale, (high * white_scale).T)
        inverses[mine, :bs, :] = packed
        inverses[mine, bs:, :] = diagonal
        return [send(inverses.at[mine], inverses.at[mine], device) for device in to_z]

    def gather_y(copies):
        for copy in copies:
            copy.wait_recv()
        span = inverses.at[pl.ds(core * 2 * depth + yy * depth, depth)]
        return send(span, span, to_y)

    def gather_core(copy):
        copy.wait_recv()
        span = inverses.at[pl.ds(core * 2 * depth, 2 * depth)]
        return send(span, span, to_core)

    def products(q):
        x_copies[q].wait_recv()

        @pl.loop(0, snaps)
        def _(position):
            pair = place_of(position, snaps)
            for n in range(2):
                i = 2 * pair + n
                chosen = jnp.concatenate([panels[q][columns_ref[i * NNZ + k]] for k in range(NNZ)], axis=0)
                x = x_ref[:, pl.ds(pl.multiple_of(i * bs, bs), bs)]
                partial[q][position, n * NNZ * part : (n + 1) * NNZ * part, :] = cross_scale * jnp.dot(
                    chosen, x, preferred_element_type=jnp.float32
                )

        return send(partial[q].at[pl.ds((1 - core) * 2 * depth, 2 * depth)], core_in[q], to_core)

    def encode(value_ref, n, code_ref, scale_ref, m):
        for g in range(2 * NNZ):
            cut = slice(g * part, (g + 1) * part)
            value = value_ref[n, cut, :]
            top = jnp.maximum(jnp.max(jnp.abs(value), axis=0, keepdims=True), 1e-30)
            code_ref[m, cut, :] = jnp.round(value * (LEVELS / top)).astype(jnp.int32).astype(jnp.int16)
            scale_ref[m, g : g + 1, :] = top * (1.0 / LEVELS)

    def decode(code_ref, scale_ref, m, g):
        code = code_ref[m, g * part : (g + 1) * part, :].astype(jnp.int32).astype(jnp.float32)
        return code * scale_ref[m, g : g + 1, :]

    def cross_to_y(q, copy):
        copy.wait_recv()
        add(core_sum[q], 2 * depth, partial[q], core * 2 * depth, core_in[q])

        @pl.loop(0, depth)
        def _(n):
            encode(core_sum[q], (1 - yy) * depth + n, y_out[q], y_out_scale[q], n)

        return [send(y_out[q], y_in[q], to_y), send(y_out_scale[q], y_in_scale[q], to_y)]

    def cross_to_z(q, copies):
        for copy in copies:
            copy.wait_recv()

        @pl.loop(0, depth)
        def _(n):
            for g in range(2 * NNZ):
                cut = slice(g * part, (g + 1) * part)
                y_sum[q][n, cut, :] = core_sum[q][yy * depth + n, cut, :] + decode(y_in[q], y_in_scale[q], n, g)
            encode(y_sum[q], n, z_out[q], z_out_scale[q], n)

        copies = []
        for m in range(1, depth):
            n = (zz + m) % depth
            copies.append(send(z_out[q].at[n], z_in[q].at[m - 1], to_z[m - 1]))
            copies.append(send(z_out_scale[q].at[n], z_in_scale[q].at[m - 1], to_z[m - 1]))
        return copies

    def cross_done(q, copies):
        for copy in copies:
            copy.wait_recv()
        for g in range(2 * NNZ):
            total = y_sum[q][zz, g * part : (g + 1) * part, :]
            for m in range(depth - 1):
                total = total + decode(z_in[q], z_in_scale[q], m, g)
            z_sum[g, q * part : (q + 1) * part, :] = total

    chain = gram_to_y()
    groups = bs // 8
    in_core, in_y, in_z = {}, {}, {}
    for q in range(chunks):
        in_core[q] = products(q)
        if q > 0:
            in_y[q - 1] = cross_to_y(q - 1, in_core[q - 1])
        if q > 1:
            in_z[q - 2] = cross_to_z(q - 2, in_y[q - 2])
        if q > 3:
            cross_done(q - 4, in_z[q - 4])
        if q == chunks // 8:
            chain = gram_to_z(chain)
        if q == chunks // 4:
            factor_start(chain)
        for turn in range(4):
            if q == chunks // 4 + turn * chunks // 8:
                eliminate(state, turn * groups // 4, (turn + 1) * groups // 4)
        if q == 5 * chunks // 8:
            chain = factor_end()
        if q == 6 * chunks // 8:
            chain = gather_y(chain)
    in_y[chunks - 1] = cross_to_y(chunks - 1, in_core[chunks - 1])
    in_z[chunks - 2] = cross_to_z(chunks - 2, in_y[chunks - 2])
    chain = gather_core(chain)
    in_z[chunks - 1] = cross_to_z(chunks - 1, in_y[chunks - 1])
    chain.wait_recv()
    inverse_ref[...] = inverses[...]
    for q in range(chunks - 4, chunks):
        cross_done(q, in_z[q])
    for n in range(2 * NNZ):
        cross_ref[n * bs : (n + 1) * bs, :] = z_sum[n].T
    for copy in started:
        copy.wait_send()


def whiten_kernel(depth, x_ref, y_ref, inverse_ref, out_ref):
    bs = inverse_ref.shape[-1]
    step = pl.program_id(0)
    row = lax.broadcasted_iota(jnp.int32, (bs, bs), 0)
    lane = lax.broadcasted_iota(jnp.int32, (bs, bs), 1)
    for n in range(4):
        position = (n % 2) * 2 * depth + (n // 2) * depth + step
        packed = inverse_ref[position, :bs, :]
        diagonal = jnp.broadcast_to(inverse_ref[position, bs : bs + 1, :], (bs, bs))
        first = jnp.where(lane >= row, packed.T, 0.0)
        second = jnp.where(lane > row, packed, jnp.where(lane == row, diagonal, 0.0))
        for m, inverse in enumerate((first, second)):
            high = inverse.astype(jnp.bfloat16)
            low = (inverse - high.astype(jnp.float32)).astype(jnp.bfloat16)
            weights = jnp.concatenate([high, low], axis=0)
            cut = slice((2 * n + m) * bs, (2 * n + m + 1) * bs)
            for k, ref in enumerate((x_ref, y_ref)):
                psi = ref[:, cut]
                out_ref[k, :, cut] = jnp.dot(
                    jnp.concatenate([psi, psi], axis=1), weights, preferred_element_type=jnp.float32
                )


CHUNKS = 8
LEVELS = 32767.0


def fast_shards(psi_x, psi_y, pattern):
    rows, width = psi_x.shape
    blocks = pattern.shape[0]
    bs = width // blocks
    snaps = lax.axis_size("snap")
    depth = snaps // 4
    total = rows * snaps
    chunks = CHUNKS
    part = bs // chunks
    columns = kept_columns(pattern)
    local = (columns + blocks * lax.axis_index("obs")) % (2 * blocks)
    f32, bf16 = jnp.float32, jnp.bfloat16
    vmem = pl.BlockSpec(memory_space=pltpu.VMEM)
    tall = bs + 8
    piece = 2 * NNZ * part
    count = chunks * (4 + 2 * (depth - 1)) + 2 * (depth + 1)
    cross, inverse = pl.pallas_call(
        functools.partial(
            window_kernel, snaps, chunks, 1.0 / math.sqrt(total), math.sqrt(2.0 * total)
        ),
        out_shape=(
            jax.ShapeDtypeStruct((2 * NNZ * bs, bs), f32),
            jax.ShapeDtypeStruct((snaps, tall, bs), f32),
        ),
        in_specs=[pl.BlockSpec(memory_space=pltpu.SMEM), vmem, vmem],
        out_specs=(vmem, vmem),
        scratch_shapes=[
            [pltpu.VMEM((2 * blocks, part, rows), bf16)] * chunks,
            [pltpu.VMEM((snaps, piece, bs), f32)] * chunks,
            [pltpu.VMEM((2 * depth, piece, bs), f32)] * chunks,
            [pltpu.VMEM((2 * depth, piece, bs), f32)] * chunks,
            [pltpu.VMEM((depth, piece, bs), jnp.int16)] * chunks,
            [pltpu.VMEM((depth, piece, bs), jnp.int16)] * chunks,
            [pltpu.VMEM((depth, piece, bs), f32)] * chunks,
            [pltpu.VMEM((depth, piece, bs), jnp.int16)] * chunks,
            [pltpu.VMEM((depth - 1, piece, bs), jnp.int16)] * chunks,
            pltpu.VMEM((2 * NNZ, bs, bs), f32),
            [pltpu.VMEM((depth, 2 * NNZ, bs), f32)] * chunks,
            [pltpu.VMEM((depth, 2 * NNZ, bs), f32)] * chunks,
            [pltpu.VMEM((depth, 2 * NNZ, bs), f32)] * chunks,
            [pltpu.VMEM((depth - 1, 2 * NNZ, bs), f32)] * chunks,
            pltpu.VMEM((snaps, tall, bs), f32),
            pltpu.VMEM((2 * depth, tall, bs), f32),
            pltpu.VMEM((2 * depth, tall, bs), f32),
            pltpu.VMEM((depth, tall, bs), f32),
            pltpu.VMEM((depth, tall, bs), f32),
            pltpu.VMEM((depth - 1, tall, bs), f32),
            pltpu.VMEM((2, bs, bs), f32),
            pltpu.VMEM((snaps, tall, bs), f32),
            pltpu.SemaphoreType.DMA((count,)),
            pltpu.SemaphoreType.DMA((count,)),
        ],
        compiler_params=pltpu.CompilerParams(
            collective_id=0, has_side_effects=True, vmem_limit_bytes=62_000_000
        ),
        name="window",
    )(local.reshape(-1), psi_x, psi_y)
    whitened = pl.pallas_call(
        functools.partial(whiten_kernel, depth),
        grid=(depth,),
        in_specs=[pl.BlockSpec((rows, 8 * bs), lambda n: (0, n))] * 2
        + [pl.BlockSpec((snaps, tall, bs), lambda n: (0, 0, 0), pipeline_mode=pl.Buffered(1))],
        out_specs=pl.BlockSpec((2, rows, 8 * bs), lambda n: (0, 0, n)),
        out_shape=jax.ShapeDtypeStruct((2, rows, width), f32),
        name="whiten",
    )(psi_x, psi_y, inverse)
    return (cross, whitened)


def shards(psi_x, psi_y, pattern):
    blocks = pattern.shape[0]
    snaps = lax.axis_size("snap")
    fits = lax.axis_size("obs") == 2 and snaps % 4 == 0 and snaps > 4 and blocks == 2 * snaps
    if fits and psi_x.shape[1] // blocks == 128 and psi_x.shape[0] % 128 == 0:
        return fast_shards(psi_x, psi_y, pattern)
    return general_shards(psi_x, psi_y, pattern)


def solution(mesh):
    placed = (P("snap", "obs"), P("snap", "obs"), P("obs", None))
    return jax.shard_map(
        shards,
        mesh=mesh,
        in_specs=placed,
        out_specs=(P(("obs", "snap"), None), P(None, "snap", "obs")),
        check_vma=False,
    )
```

profile of v0, /device:TPU:0, one launch (start us, length us, event | category | flops | bytes accessed | tf_op | source)
XLA Modules:
  0.0 95.3 jit_solution(4360167540480596950)
XLA Ops:
  0.7 0.9 convolution_bitcast_fusion
  1.6 0.2 convert_reduce_fusion
  1.8 0.1 copy.5
  1.9 0.1 add.39
  2.0 0.5 and_select_fusion.columns_ref
  2.5 84.3 %window.1 = (f32[1024,128]{1,0:T(8,128)}, f32[16,136,128]{2,1,0:T(8,128)}) custom-call(s32[128]{0:T(128)} %and_select_fusion.columns_ref, bf16[256,4096]{1,0:T(8,128)(2,1)} %x_ref.3, bf16[256,4096]{1,0:T(8,128)(2,1)} %y_ref.3), custom_call_target="tpu_custom_call" | custom-call | tf_op jit(solution)/shard_map/window/pallas_call | solution.py:403
  86.8 0.0 copy-start
  86.8 7.6 %whiten.1 = f32[2,256,4096]{2,1,0:T(8,128)} custom-call(bf16[256,4096]{1,0:T(8,128)(2,1)} %x_ref.3, bf16[256,4096]{1,0:T(8,128)(2,1)} %y_ref.3, f32[16,136,128]{2,1,0:T(8,128)} %get-tuple-element.5.inverse_ref), custom_call_target="tpu_custom_call" | custom-call | tf_op jit(solution)/shard_map/whiten/pallas_call | solution.py:444
  94.5 0.0 copy-done
  94.5 0.8 copy.7
  (3 shorter events, 0.0 us)
Async XLA Ops:
  86.8 7.7 %copy-start = (f32[1024,128]{1,0:T(8,128)S(1)}, f32[1024,128]{1,0:T(8,128)}, u32[]{:S(2)}) copy-start(f32[1024,128]{1,0:T(8,128)} %get-tuple-element.8) | copy-start | bytes 1572868
where the time goes:
time: 95.5 us; the launch traced here: 95.3 us
  Pallas kernels  91.9 us (96%)
  local copies, waits for them, and re-layouts  1 us (1%)
    pallas_call x1, Pallas kernels, fast_shards(): pl.pallas_call(functools.partial(window_kernel, snaps, chunks, 1.0 / math...  84.3 us
    pallas_call x1, Pallas kernels, fast_shards(): pl.pallas_call(functools.partial(whiten_kernel, depth), grid=(depth,), in...  7.64 us

commit v1 on v0

--- a/solution.py
+++ b/solution.py
@@ -82,14 +82,6 @@
     return lax.dot_general(a, b, (((0,), (0,)), ((), ())), preferred_element_type=jnp.float32)
 
 
-def kept_columns(pattern):
-    total = pattern.shape[1]
-    upper = jnp.triu(jnp.ones((total, total), jnp.bfloat16))
-    counts = jnp.dot(pattern.astype(jnp.bfloat16), upper, preferred_element_type=jnp.float32)
-    slots = jnp.arange(NNZ, dtype=jnp.float32)
-    return jnp.sum((counts[:, None, :] <= slots[None, :, None] + 0.5).astype(jnp.int32), axis=2)
-
-
 def place_of(position, snaps):
     depth = snaps // 4
     return (position % depth) * 4 + ((position // depth) % 2) * 2 + position // (2 * depth)
@@ -116,7 +108,7 @@
             for block in blocks:
                 pivot = 1.0 / block[0][r : r + 1, r : r + 1]
                 scaled = jnp.where(at_lane[:1], pivot, block[0][r : r + 1, :] * pivot)
-                for v in range(slab_count):
+                for v in range(slab_count - first):
                     column = jnp.broadcast_to(block[v][:, r : r + 1], (8, bs))
                     updated = jnp.where(at_lane, 0.0, block[v]) - column * scaled
                     if v == 0:
@@ -144,13 +136,34 @@
     return unit * (1.0 / jnp.sqrt(pivot))
 
 
+def column_table(pattern, side):
+    count, total = pattern.shape
+    row = lax.broadcasted_iota(jnp.int32, (total, total), 0)
+    lane = lax.broadcasted_iota(jnp.int32, (total, total), 1)
+    upper = jnp.where(row <= lane, 1.0, 0.0).astype(jnp.bfloat16)
+    counts = jnp.dot(
+        pattern.astype(jnp.float32).astype(jnp.bfloat16), upper, preferred_element_type=jnp.float32
+    )
+    slot = lax.broadcasted_iota(jnp.int32, (count, 128), 1)
+    found = jnp.zeros((count, 128), jnp.int32)
+    for k in range(NNZ):
+        before = jnp.sum(jnp.where(counts <= k + 0.5, 1.0, 0.0), axis=1, keepdims=True)
+        found = jnp.where(slot == k, jnp.broadcast_to(before, (count, 128)).astype(jnp.int32), found)
+    found = found + (total // 2) * side
+    return jnp.where(found >= total, found - total, found)
+
+
+def columns_kernel(pattern_ref, columns_ref):
+    columns_ref[...] = column_table(pattern_ref[...], lax.axis_index("obs"))
+
+
 def window_kernel(
     snaps, chunks, cross_scale, white_scale,
-    columns_ref, x_ref, y_ref, cross_ref, inverse_ref,
+    columns_ref, x_hbm, y_hbm, cross_ref, white_ref, x_ref, y_ref,
     panels, partial, core_in, core_sum, y_out, y_in, y_sum, z_out, z_in, z_sum,
     y_out_scale, y_in_scale, z_out_scale, z_in_scale,
     gram, gram_core, gram_sum, gram_y, gram_ysum, gram_z, state, inverses,
-    send_sem, recv_sem,
+    load_sem, send_sem, recv_sem,
 ):
     rows, width = x_ref.shape
     bs = cross_ref.shape[1]
@@ -165,12 +178,51 @@
     to_y = (side, here + 2 - 4 * yy)
     to_z = [(side, (here + 4 * m) % snaps) for m in range(1, depth)]
     mine = core * 2 * depth + yy * depth + zz
+    pieces = 4
+    per = blocks // pieces
 
     barrier = pltpu.get_barrier_semaphore()
     others = [to_x, to_core, to_y] + to_z
     for device in others:
         pl.semaphore_signal(barrier, inc=1, device_id=device, device_id_type=pl.DeviceIdType.MESH)
-    pl.semaphore_wait(barrier, len(others))
+
+    loads = []
+    for n in range(pieces):
+        cut = pl.ds(n * per * bs, per * bs)
+        loads.append(pltpu.make_async_copy(y_hbm.at[:, cut], y_ref.at[:, cut], load_sem.at[n]))
+    x_load = pltpu.make_async_copy(x_hbm, x_ref, load_sem.at[pieces])
+    for copy in loads + [x_load]:
+        copy.start()
+
+    for n in range(pieces):
+        loads[n].wait()
+
+        @pl.loop(n * per, (n + 1) * per)
+        def _(j):
+            turned = y_ref[:, pl.ds(pl.multiple_of(j * bs, bs), bs)].T
+            for q in range(chunks):
+                panels[q][j] = turned[q * part : (q + 1) * part]
+
+    half = 2 * depth
+    away, home = (1 - core) * half, core * half
+
+    x_load.wait()
+
+    def gram_pairs(first):
+        @pl.loop(0, half, unroll=GRAM_UNROLL)
+        def _(n):
+            position = first + n
+            pair = place_of(position, snaps)
+            found = []
+            for m in range(2):
+                cut = pl.ds(pl.multiple_of((2 * pair + m) * bs, bs), bs)
+                both = jnp.concatenate([x_ref[:, cut], y_ref[:, cut]], axis=0)
+                found.append(dot_rows(both, both))
+            packed, diagonal = pack_pair(*found)
+            gram[position, :bs, :] = packed
+            gram[position, bs:, :] = diagonal
+
+    gram_pairs(away)
 
     started = []
 
@@ -184,38 +236,23 @@
         started.append(copy)
         return copy
 
-    @pl.loop(0, blocks)
-    def _(j):
-        turned = y_ref[:, pl.ds(pl.multiple_of(j * bs, bs), bs)].T
-        for q in range(chunks):
-            panels[q][j] = turned[q * part : (q + 1) * part]
-
+    pl.semaphore_wait(barrier, len(others))
     x_copies = [
         send(panels[q].at[pl.ds(0, blocks)], panels[q].at[pl.ds(blocks, blocks)], to_x) for q in range(chunks)
     ]
 
-    @pl.loop(0, snaps)
-    def _(position):
-        pair = place_of(position, snaps)
-        found = []
-        for n in range(2):
-            cut = pl.ds(pl.multiple_of((2 * pair + n) * bs, bs), bs)
-            both = jnp.concatenate([x_ref[:, cut], y_ref[:, cut]], axis=0)
-            found.append(dot_rows(both, both))
-        packed, diagonal = pack_pair(*found)
-        gram[position, :bs, :] = packed
-        gram[position, bs:, :] = diagonal
 
     def add(out, count, a, a_first, b):
-        @pl.loop(0, count)
+        @pl.loop(0, count, unroll=2)
         def _(n):
             out[n] = a[a_first + n] + b[n]
 
-    gram_copy = send(gram.at[pl.ds((1 - core) * 2 * depth, 2 * depth)], gram_core, to_core)
+    gram_copy = send(gram.at[pl.ds(away, half)], gram_core, to_core)
+    gram_pairs(home)
 
     def gram_to_y():
         gram_copy.wait_recv()
-        add(gram_sum, 2 * depth, gram, core * 2 * depth, gram_core)
+        add(gram_sum, half, gram, home, gram_core)
         return send(gram_sum.at[pl.ds((1 - yy) * depth, depth)], gram_y, to_y)
 
     def gram_to_z(copy):
@@ -248,29 +285,48 @@
     def gather_y(copies):
         for copy in copies:
             copy.wait_recv()
-        span = inverses.at[pl.ds(core * 2 * depth + yy * depth, depth)]
+        span = inverses.at[pl.ds(home + yy * depth, depth)]
         return send(span, span, to_y)
 
     def gather_core(copy):
         copy.wait_recv()
-        span = inverses.at[pl.ds(core * 2 * depth, 2 * depth)]
+        span = inverses.at[pl.ds(home, half)]
         return send(span, span, to_core)
 
-    def products(q):
-        x_copies[q].wait_recv()
-
-        @pl.loop(0, snaps)
-        def _(position):
+    def whiten(first, count):
+        @pl.loop(0, count, unroll=WHITE_UNROLL)
+        def _(n):
+            position = first + n
             pair = place_of(position, snaps)
-            for n in range(2):
-                i = 2 * pair + n
-                chosen = jnp.concatenate([panels[q][columns_ref[i * NNZ + k]] for k in range(NNZ)], axis=0)
+            row = lax.broadcasted_iota(jnp.int32, (bs, bs), 0)
+            lane = lax.broadcasted_iota(jnp.int32, (bs, bs), 1)
+            packed = inverses[position, :bs, :]
+            diagonal = jnp.broadcast_to(inverses[position, bs : bs + 1, :], (bs, bs))
+            first_block = jnp.where(lane >= row, packed.T, 0.0)
+            second_block = jnp.where(lane > row, packed, jnp.where(lane == row, diagonal, 0.0))
+            for m, inverse in enumerate((first_block, second_block)):
+                high = inverse.astype(jnp.bfloat16)
+                low = (inverse - high.astype(jnp.float32)).astype(jnp.bfloat16)
+                weights = jnp.concatenate([high, low], axis=0)
+                cut = pl.ds(pl.multiple_of((2 * pair + m) * bs, bs), bs)
+                for k, ref in enumerate((x_ref, y_ref)):
+                    psi = ref[:, cut]
+                    white_ref[k, :, cut] = jnp.dot(
+                        jnp.concatenate([psi, psi], axis=1), weights, preferred_element_type=jnp.float32
+                    )
+
+    def products(q, first):
+        @pl.loop(0, half, unroll=PRODUCT_UNROLL)
+        def _(n):
+            position = first + n
+            pair = place_of(position, snaps)
+            for m in range(2):
+                i = 2 * pair + m
+                chosen = jnp.concatenate([panels[q][columns_ref[i, k]] for k in range(NNZ)], axis=0)
                 x = x_ref[:, pl.ds(pl.multiple_of(i * bs, bs), bs)]
-                partial[q][position, n * NNZ * part : (n + 1) * NNZ * part, :] = cross_scale * jnp.dot(
+                partial[q][position, m * NNZ * part : (m + 1) * NNZ * part, :] = cross_scale * jnp.dot(
                     chosen, x, preferred_element_type=jnp.float32
                 )
-
-        return send(partial[q].at[pl.ds((1 - core) * 2 * depth, 2 * depth)], core_in[q], to_core)
 
     def encode(value_ref, n, code_ref, scale_ref, m):
         for g in range(2 * NNZ):
@@ -284,11 +340,18 @@
         code = code_ref[m, g * part : (g + 1) * part, :].astype(jnp.int32).astype(jnp.float32)
         return code * scale_ref[m, g : g + 1, :]
 
+    def cross_to_core(q):
+        x_copies[q].wait_recv()
+        products(q, away)
+        copy = send(partial[q].at[pl.ds(away, half)], core_in[q], to_core)
+        products(q, home)
+        return copy
+
     def cross_to_y(q, copy):
         copy.wait_recv()
-        add(core_sum[q], 2 * depth, partial[q], core * 2 * depth, core_in[q])
-
-        @pl.loop(0, depth)
+        add(core_sum[q], half, partial[q], home, core_in[q])
+
+        @pl.loop(0, depth, unroll=CODE_UNROLL)
         def _(n):
             encode(core_sum[q], (1 - yy) * depth + n, y_out[q], y_out_scale[q], n)
 
@@ -298,7 +361,7 @@
         for copy in copies:
             copy.wait_recv()
 
-        @pl.loop(0, depth)
+        @pl.loop(0, depth, unroll=CODE_UNROLL)
         def _(n):
             for g in range(2 * NNZ):
                 cut = slice(g * part, (g + 1) * part)
@@ -321,35 +384,40 @@
                 total = total + decode(z_in[q], z_in_scale[q], m, g)
             z_sum[g, q * part : (q + 1) * part, :] = total
 
+    groups = bs // 8
     chain = gram_to_y()
-    groups = bs // 8
-    in_core, in_y, in_z = {}, {}, {}
+    in_y, in_z = {}, {}
     for q in range(chunks):
-        in_core[q] = products(q)
-        if q > 0:
-            in_y[q - 1] = cross_to_y(q - 1, in_core[q - 1])
+        in_core = cross_to_core(q)
+        if q == 2:
+            in_z[0] = cross_to_z(0, in_y[0])
         if q > 1:
-            in_z[q - 2] = cross_to_z(q - 2, in_y[q - 2])
-        if q > 3:
-            cross_done(q - 4, in_z[q - 4])
-        if q == chunks // 8:
+            in_z[q - 1] = cross_to_z(q - 1, in_y[q - 1])
+        in_y[q] = cross_to_y(q, in_core)
+        if q > 2:
+            cross_done(q - 3, in_z[q - 3])
+        if q == GRAM_Z:
             chain = gram_to_z(chain)
-        if q == chunks // 4:
+        if q == FACTOR:
             factor_start(chain)
-        for turn in range(4):
-            if q == chunks // 4 + turn * chunks // 8:
-                eliminate(state, turn * groups // 4, (turn + 1) * groups // 4)
-        if q == 5 * chunks // 8:
+            eliminate(state, 0, groups // 4)
+            eliminate(state, groups // 4, groups // 2)
+        if q == FACTOR + 1:
+            eliminate(state, groups // 2, 3 * groups // 4)
+            eliminate(state, 3 * groups // 4, groups)
             chain = factor_end()
-        if q == 6 * chunks // 8:
+        if q == GATHER_Y:
             chain = gather_y(chain)
-    in_y[chunks - 1] = cross_to_y(chunks - 1, in_core[chunks - 1])
-    in_z[chunks - 2] = cross_to_z(chunks - 2, in_y[chunks - 2])
-    chain = gather_core(chain)
-    in_z[chunks - 1] = cross_to_z(chunks - 1, in_y[chunks - 1])
+            whiten(home + yy * depth, depth)
+        if q == GATHER_CORE:
+            chain = gather_core(chain)
+            whiten(home + (1 - yy) * depth, depth)
+    last = chunks - 1
     chain.wait_recv()
-    inverse_ref[...] = inverses[...]
-    for q in range(chunks - 4, chunks):
+    whiten(away, depth)
+    in_z[last] = cross_to_z(last, in_y[last])
+    whiten(away + depth, depth)
+    for q in range(last - 2, chunks):
         cross_done(q, in_z[q])
     for n in range(2 * NNZ):
         cross_ref[n * bs : (n + 1) * bs, :] = z_sum[n].T
@@ -357,27 +425,9 @@
         copy.wait_send()
 
 
-def whiten_kernel(depth, x_ref, y_ref, inverse_ref, out_ref):
-    bs = inverse_ref.shape[-1]
-    step = pl.program_id(0)
-    row = lax.broadcasted_iota(jnp.int32, (bs, bs), 0)
-    lane = lax.broadcasted_iota(jnp.int32, (bs, bs), 1)
-    for n in range(4):
-        position = (n % 2) * 2 * depth + (n // 2) * depth + step
-        packed = inverse_ref[position, :bs, :]
-        diagonal = jnp.broadcast_to(inverse_ref[position, bs : bs + 1, :], (bs, bs))
-        first = jnp.where(lane >= row, packed.T, 0.0)
-        second = jnp.where(lane > row, packed, jnp.where(lane == row, diagonal, 0.0))
-        for m, inverse in enumerate((first, second)):
-            high = inverse.astype(jnp.bfloat16)
-            low = (inverse - high.astype(jnp.float32)).astype(jnp.bfloat16)
-            weights = jnp.concatenate([high, low], axis=0)
-            cut = slice((2 * n + m) * bs, (2 * n + m + 1) * bs)
-            for k, ref in enumerate((x_ref, y_ref)):
-                psi = ref[:, cut]
-                out_ref[k, :, cut] = jnp.dot(
-                    jnp.concatenate([psi, psi], axis=1), weights, preferred_element_type=jnp.float32
-                )
+GRAM_Z, FACTOR, GATHER_Y, GATHER_CORE = 0, 2, 5, 7
+
+PRODUCT_UNROLL, GRAM_UNROLL, WHITE_UNROLL, CODE_UNROLL = 8, 4, 4, 4
 
 
 CHUNKS = 8
@@ -393,24 +443,32 @@
     total = rows * snaps
     chunks = CHUNKS
     part = bs // chunks
-    columns = kept_columns(pattern)
-    local = (columns + blocks * lax.axis_index("obs")) % (2 * blocks)
     f32, bf16 = jnp.float32, jnp.bfloat16
     vmem = pl.BlockSpec(memory_space=pltpu.VMEM)
+    hbm = pl.BlockSpec(memory_space=pltpu.HBM)
     tall = bs + 8
     piece = 2 * NNZ * part
     count = chunks * (4 + 2 * (depth - 1)) + 2 * (depth + 1)
-    cross, inverse = pl.pallas_call(
+    columns = pl.pallas_call(
+        columns_kernel,
+        out_shape=jax.ShapeDtypeStruct((blocks, 128), jnp.int32),
+        in_specs=[vmem],
+        out_specs=vmem,
+        name="columns",
+    )(pattern)
+    return pl.pallas_call(
         functools.partial(
             window_kernel, snaps, chunks, 1.0 / math.sqrt(total), math.sqrt(2.0 * total)
         ),
         out_shape=(
             jax.ShapeDtypeStruct((2 * NNZ * bs, bs), f32),
-            jax.ShapeDtypeStruct((snaps, tall, bs), f32),
+            pltpu.VMEM((2, rows, width), f32),
         ),
-        in_specs=[pl.BlockSpec(memory_space=pltpu.SMEM), vmem, vmem],
+        in_specs=[pl.BlockSpec(memory_space=pltpu.SMEM), hbm, hbm],
         out_specs=(vmem, vmem),
         scratch_shapes=[
+            pltpu.VMEM((rows, width), bf16),
+            pltpu.VMEM((rows, width), bf16),
             [pltpu.VMEM((2 * blocks, part, rows), bf16)] * chunks,
             [pltpu.VMEM((snaps, piece, bs), f32)] * chunks,
             [pltpu.VMEM((2 * depth, piece, bs), f32)] * chunks,
@@ -433,24 +491,15 @@
             pltpu.VMEM((depth - 1, tall, bs), f32),
             pltpu.VMEM((2, bs, bs), f32),
             pltpu.VMEM((snaps, tall, bs), f32),
+            pltpu.SemaphoreType.DMA((5,)),
             pltpu.SemaphoreType.DMA((count,)),
             pltpu.SemaphoreType.DMA((count,)),
         ],
         compiler_params=pltpu.CompilerParams(
-            collective_id=0, has_side_effects=True, vmem_limit_bytes=62_000_000
+            collective_id=0, has_side_effects=True, vmem_limit_bytes=46_000_000
         ),
         name="window",
-    )(local.reshape(-1), psi_x, psi_y)
-    whitened = pl.pallas_call(
-        functools.partial(whiten_kernel, depth),
-        grid=(depth,),
-        in_specs=[pl.BlockSpec((rows, 8 * bs), lambda n: (0, n))] * 2
-        + [pl.BlockSpec((snaps, tall, bs), lambda n: (0, 0, 0), pipeline_mode=pl.Buffered(1))],
-        out_specs=pl.BlockSpec((2, rows, 8 * bs), lambda n: (0, 0, n)),
-        out_shape=jax.ShapeDtypeStruct((2, rows, width), f32),
-        name="whiten",
-    )(psi_x, psi_y, inverse)
-    return (cross, whitened)
+    )(columns, *[pltpu.with_memory_space_constraint(a, pltpu.HBM) for a in (psi_x, psi_y)])
 
 
 def shards(psi_x, psi_y, pattern):

time: 95.5 us -> 86.4 us (0.905)
  Pallas kernels: 91.9 us -> 80.5 us
  local copies, waits for them, and re-layouts: 1 us -> 4.91 us
    pallas_call x1, Pallas kernels: 7.64 us -> 1.54 us  [fast_shards(): pl.pallas_call(columns_kernel, out_shape=jax.ShapeDtypeStruct((blocks, 12...]
    pallas_call x1, Pallas kernels: 84.3 us -> 79 us  [fast_shards(): pl.pallas_call(functools.partial(window_kernel, snaps, chunks, 1.0 / math...]
    unnamed x3 -> x4, local copies, waits for them, and re-layouts: 0.8 us -> 4.91 us
where the time goes in v1:
time: 86.4 us; the launch traced here: 86.1 us
  Pallas kernels  80.5 us (93%)
  local copies, waits for them, and re-layouts  4.91 us (6%)
    pallas_call x1, Pallas kernels, fast_shards(): pl.pallas_call(functools.partial(window_kernel, snaps, chunks, 1.0 / math...  79 us
    unnamed x4, local copies, waits for them, and re-layouts  4.91 us

profile of v1, /device:TPU:0, one launch (start us, length us, event | category | flops | bytes accessed | tf_op | source)
XLA Modules:
  0.0 86.1 jit_solution(11652799667911842769)
XLA Ops:
  0.6 1.5 %columns.1.columns_ref = s32[32,128]{1,0:T(8,128)} custom-call(s32[32,64]{1,0:T(8,128)} %pattern_ref.1), custom_call_target="tpu_custom_call" | custom-call | tf_op jit(solution)/shard_map/columns/pallas_call | solution.py:452
  2.2 0.0 copy-start
  2.2 0.7 copy-done
  2.9 79.0 %window.1 = (f32[1024,128]{1,0:T(8,128)S(1)}, f32[2,256,4096]{2,1,0:T(8,128)S(1)}) custom-call(s32[32,128]{1,0:T(8,128)S(1)} %copy-done, bf16[256,4096]{1,0:T(8,128)(2,1)} %x_hbm.1, bf16[256,4096]{1,0:T(8,128)(2,1)} %y_hbm.1), custom_call_target="tpu_custom_call" | custom-call | tf_op jit(solution)/shard_map/window/pallas_call | solution.py:459
  81.9 3.4 %copy.7 = f32[2,256,4096]{2,1,0:T(8,128)} copy(f32[2,256,4096]{2,1,0:T(8,128)S(1)} %get-tuple-element.3) | data formatting | bytes 16777216
  85.3 0.8 copy.8
Async XLA Ops:
  2.2 0.7 copy-start
